TPU v7x, 32 devices: a whole 2x2x4 slice. The times are simulated.
32 devices in a mesh: exp: 4 (over z), tile: 8 (over y, x, core).
Axes of the slice: x: 2, y: 2, z: 4, core: 2. Of those that a mesh axis runs over, the one named last changes fastest.
Arguments:
- science: bfloat16 [4, 8, 128, 256], P('exp', 'tile'), may hold values from -6 to 6
- mask_bits: int32 [4, 8, 128, 256], P('exp', 'tile'), may hold values from 0 to 1023, as said below
- variance: bfloat16 [4, 8, 128, 256], P('exp', 'tile'), may hold values from 0.25 to 4
- kernel_poly: float32 [4, 8, 8, 3], P('exp', 'tile'), may hold values from -5 to 5
- basis_rows: bfloat16 [8, 31], replicated, may hold values from -1 to 1
- basis_cols: bfloat16 [8, 31], replicated, may hold values from -1 to 1
- destination: int32 [4, 8, 16, 1], P('exp', 'tile'), may hold values from 0 to 7, as said below
- row_offset: int32 [4, 8, 16], P('exp', 'tile'), may hold values from 0 to 1023, as said below
Outputs:
- template: bfloat16 [8192, 128], P('tile')
- difference: bfloat16 [4, 8, 128, 256], P('exp', 'tile')
Inputs may be any that keep to these rules, and one draw needn't show every extreme that they name: `destination`: the pieces of the CCD region at tile index t land, in order of piece number, in contiguous runs on tiles t, t + 1 and t + 2 modulo 8; at most 8 pieces of one region land in one tile, and in every draw some region has exactly 8 in one tile. `row_offset`: offsets of consecutive rows of pieces mostly rise by about 16, wrapping within a tile. `mask_bits`: A pixel is rejected where any of bits 0, 1 or 2 is set; only bits 0 to 9 are used, and in every draw some pixel has all ten set.
All inputs are finite; a program needn't handle non-finite values.
Results may differ from a plain program's by a relative error of at most 0.0063.
Values may be sent and summed in bfloat16 or wider, within the bound.
No kernel may reach another device: no remote copies, remote signals or barrier semaphores. Data moves between devices by JAX's collectives and lax.ppermute only.
A program may use at most 64 MiB of HBM per device.

v0:
```python
import jax
import jax.numpy as jnp
from jax import lax
from jax.sharding import PartitionSpec as P

PR = 16
PC = 128
TR = 1024


def shifted(shard, axis, by):
    length = lax.axis_size(axis)
    return lax.ppermute(shard, axis, [(i, (i + by) % length) for i in range(length)])


def padded_2(cells, sides, width):
    for axis, dim in sides:
        count = lax.axis_size(axis)
        ends = count - 1
        head = lax.slice_in_dim(cells, 0, width, axis=dim)
        tail = lax.slice_in_dim(cells, cells.shape[dim] - width, cells.shape[dim], axis=dim)
        cells = jnp.concatenate(
            [
                lax.ppermute(tail, axis, [(i, (i + 1) % count) for i in range(ends)]),
                cells,
                lax.ppermute(head, axis, [((i + 1) % count, i) for i in range(ends)]),
            ],
            axis=dim,
        )
    return cells


def toeplitz(kernel_taps, length):
    half_width = kernel_taps.shape[1] // 2
    position = jnp.arange(length, dtype=jnp.int32)
    offset_index = position[:, None] - position[None, :] + half_width
    inside = (offset_index >= 0) & (offset_index < kernel_taps.shape[1])
    tap_index = jnp.where(inside, offset_index, 0)
    band_table = jnp.take(kernel_taps, tap_index, axis=1)
    return jnp.where(inside[None], band_table, jnp.zeros_like(band_table))


def coefficient_maps(kernel_terms, height, across):
    y_norm = (jnp.arange(height, dtype=jnp.int32).astype(jnp.float32) - (height - 1) / 2.0) / (
        height / 2.0
    )
    x_norm = (jnp.arange(across, dtype=jnp.int32).astype(jnp.float32) - (across - 1) / 2.0) / (
        across / 2.0
    )
    return (
        kernel_terms[:, 0, None, None]
        + kernel_terms[:, 1, None, None] * y_norm[None, :, None]
        + kernel_terms[:, 2, None, None] * x_norm[None, None, :]
    )


def send_along(bundle, step):
    return shifted((bundle[0], bundle[1], bundle[2]), "tile", step)


def send_back(bundle, step):
    return shifted(bundle, "tile", -step)


def body(
    science, mask_bits, variance, kernel_poly, basis_rows, basis_cols, destination, row_offset
):
    region = science[0, 0]
    height, across = region.shape
    col_band = toeplitz(basis_cols, across)
    row_band = toeplitz(basis_rows, height)
    first_pass = jnp.einsum(
        "yc,bcx->byx", region, col_band, preferred_element_type=jnp.float32
    ).astype(jnp.bfloat16)
    second_pass = jnp.einsum(
        "biy,bix->byx", row_band, first_pass, preferred_element_type=jnp.float32
    )
    matched = jnp.sum(coefficient_maps(kernel_poly[0, 0], height, across) * second_pass, axis=0)
    rejected = jnp.bitwise_and(mask_bits[0, 0], 7) != 0
    weight = jnp.where(rejected, jnp.float32(0.0), 1.0 / variance[0, 0].astype(jnp.float32))
    weighted = (matched * weight).astype(jnp.bfloat16)
    weight_sent = weight.astype(jnp.bfloat16)
    block_rows = height // PR
    block_cols = across // PC

    def to_pieces(picture):
        return (
            picture.reshape(block_rows, PR, block_cols, PC)
            .transpose(0, 2, 1, 3)
            .reshape(-1, PR, PC)
        )

    target = destination.reshape(-1)
    offset = row_offset.reshape(-1)
    pieces_count = target.shape[0]
    tile_count = lax.axis_size("tile")
    reach = 3
    slot_count = pieces_count // 2
    slot_total = reach * slot_count
    offset = jnp.where(target == tile_count - 1, jnp.minimum(offset, TR - PR), offset)
    relative = (target - lax.axis_index("tile") + tile_count) % tile_count
    one_hot = (relative[:, None] == jnp.arange(reach, dtype=jnp.int32)[None, :]).astype(jnp.int32)
    earlier = jnp.cumsum(one_hot, axis=0) - one_hot
    slot_rank = jnp.sum(earlier * one_hot, axis=1)
    send_index = relative * slot_count + slot_rank
    send_pixels = (
        jnp.zeros((slot_total, PR, PC), jnp.bfloat16).at[send_index].set(to_pieces(weighted))
    )
    send_weights = (
        jnp.zeros((slot_total, PR, PC), jnp.bfloat16).at[send_index].set(to_pieces(weight_sent))
    )
    send_offsets = jnp.full((slot_total,), -1, jnp.int32).at[send_index].set(offset)
    send_pixels = send_pixels.reshape(reach, slot_count, PR, PC)
    send_weights = send_weights.reshape(reach, slot_count, PR, PC)
    send_offsets = send_offsets.reshape(reach, slot_count)
    got_list = [(send_pixels[0], send_weights[0], send_offsets[0])]
    for step in range(1, reach):
        got_list.append(
            send_along((send_pixels[step], send_weights[step], send_offsets[step]), step)
        )
    got_pixels = jnp.stack([item[0] for item in got_list])
    got_weights = jnp.stack([item[1] for item in got_list])
    got_offsets = jnp.stack([item[2] for item in got_list])
    extent = TR + PR
    is_live = got_offsets >= 0
    sky_row = jnp.where(
        is_live[..., None], got_offsets[..., None] + jnp.arange(PR, dtype=jnp.int32), extent - 1
    ).reshape(-1)
    pixel_sum = (
        jnp.zeros((extent, PC), jnp.float32)
        .at[sky_row]
        .add(got_pixels.reshape(-1, PC).astype(jnp.float32))
    )
    weight_sum = (
        jnp.zeros((extent, PC), jnp.float32)
        .at[sky_row]
        .add(got_weights.reshape(-1, PC).astype(jnp.float32))
    )
    local_sums = jnp.stack([pixel_sum, weight_sum])[:, : extent - 1]
    rim_rows = PR - 1
    padded = padded_2(local_sums, (("tile", 1),), rim_rows)
    core_rows = padded[:, rim_rows : rim_rows + extent - 1]
    core_rows = core_rows.at[:, :rim_rows].add(padded[:, :rim_rows])
    core_rows = core_rows.at[:, TR : TR + rim_rows].add(padded[:, rim_rows + extent - 1 :])
    extended = jnp.concatenate([core_rows, jnp.zeros((2, 1, PC), jnp.float32)], axis=1)
    totals = lax.psum(extended, "exp")
    template_ext = (totals[0] / jnp.maximum(totals[1], 1.0)).astype(jnp.bfloat16)
    cutout = template_ext[sky_row].reshape(reach, slot_count, PR, PC)
    returned_list = [cutout[0]]
    for step in range(1, reach):
        returned_list.append(send_back(cutout[step], step))
    returned = jnp.stack(returned_list)
    own_cutouts = returned.reshape(slot_total, PR, PC)[send_index]
    back_image = (
        own_cutouts.reshape(block_rows, block_cols, PR, PC)
        .transpose(0, 2, 1, 3)
        .reshape(height, across)
    )
    difference = (matched - back_image.astype(jnp.float32)).astype(jnp.bfloat16)
    return (template_ext[:TR], difference[None, None])


def solution(mesh):
    placed = (
        P("exp", "tile", None, None),
        P("exp", "tile", None, None),
        P("exp", "tile", None, None),
        P("exp", "tile", None, None),
        P(),
        P(),
        P("exp", "tile", None, None),
        P("exp", "tile", None),
    )
    return jax.shard_map(
        body,
        mesh=mesh,
        in_specs=placed,
        out_specs=(P("tile", None), P("exp", "tile", None, None)),
        check_vma=False,
    )
```

profile of v0, /device:TPU:0, one launch (start us, length us, event | category | flops | bytes accessed | tf_op | source)
XLA Modules:
  0.0 417.3 jit_solution(487939907609007611)
XLA Ops:
  7.2 0.7 bitcast_select_fusion
  8.2 0.7 fusion.64
  8.9 0.6 scatter_custom_fusion
  9.6 0.5 collective-permute-start
  10.1 2.5 collective-permute-start.1
  12.9 0.7 copy.30
  13.9 228.9 %gather_fusion.1 = bf16[65536,8]{1,0:T(8,128)(2,1)} fusion(bf16[8,31]{0,1:T(8,128)(2,1)S(1)} %copy.22, s32[65536]{0:T(1024)S(1)} %broadcast_clamp_fusion), kind=kCustom, calls=%fused_computation.1 | custom fusion | bytes 2359296 | tf_op jit(solution)/shard_map/jit(_take)/gather | solution.py:39
  242.8 15.9 %copy.23 = bf16[256,256,8]{0,1,2:T(8,128)(2,1)S(1)} copy(bf16[256,256,8]{2,1,0:T(8,128)(2,1)} %bitcast.92) | data formatting | bytes 2097152 | tf_op jit(solution)/shard_map/jit(_take)/gather | solution.py:39
  258.8 57.8 %gather_fusion = bf16[16384,8]{1,0:T(8,128)(2,1)} fusion(bf16[8,31]{0,1:T(8,128)(2,1)S(1)} %copy.20, s32[16384]{0:T(1024)S(1)} %fusion.44), kind=kCustom, calls=%fused_computation | custom fusion | bytes 589824 | tf_op jit(solution)/shard_map/jit(_take)/gather | solution.py:39
  316.6 6.3 %copy.21 = bf16[128,128,8]{0,1,2:T(8,128)(2,1)S(1)} copy(bf16[128,128,8]{2,1,0:T(8,128)(2,1)} %bitcast.99) | data formatting | bytes 524288 | tf_op jit(solution)/shard_map/jit(_take)/gather | solution.py:39
  323.1 0.8 fusion
  324.3 1.0 scatter_fusion.1
  325.3 1.3 collective-permute-start.4
  326.6 1.5 collective-permute-start.5
  328.2 1.0 scatter_fusion
  329.9 1.6 collective-permute-done.5
  331.5 2.3 scatter_custom_fusion.4
  334.2 2.3 scatter_custom_fusion.2
  336.5 1.8 collective-permute-start.6
  338.4 0.8 collective-permute-done.6
  339.2 1.3 collective-permute-start.7
  340.8 1.5 collective-permute-done.7
  342.3 1.1 concatenate.11
  343.4 56.9 %all-reduce.3.cloned.1.call-done = f32[2,1040,128]{2,1,0:T(8,128)} async-done(((f32[2,1040,128]{2,1,0:T(8,128)}), f32[2,1040,128]{2,1,0:T(8,128)}) %all-reduce.3.cloned.1.call-update) | async-done | bytes 1064976 | tf_op jit(solution)/shard_map/psum | solution.py:146
  400.3 1.4 fusion.74
  401.6 1.4 gather_fusion.2
  403.1 2.0 collective-permute-start.8
  405.1 0.6 collective-permute-start.9
  405.7 0.7 slice_bitcast_fusion
  406.9 2.1 collective-permute-done.9
  409.0 0.6 gather_fusion.3
  409.8 0.6 fusion.39
  (69 shorter events, 3.6 us)
Async XLA Ops:
  7.2 315.9 %copy-start = (bf16[1,1,128,256]{3,2,1,0:T(8,128)(2,1)S(1)}, bf16[1,1,128,256]{3,2,1,0:T(8,128)(2,1)}, u32[]{:S(2)}) copy-start(bf16[1,1,128,256]{3,2,1,0:T(8,128)(2,1)} %param.12) | copy-start | bytes 196612
  7.2 6.6 %copy-start.4 = (bf16[8,31]{1,0:T(8,128)(2,1)S(1)}, bf16[8,31]{1,0:T(8,128)(2,1)}, u32[]{:S(2)}) copy-start(bf16[8,31]{1,0:T(8,128)(2,1)} %param.17) | copy-start | bytes 1492
  7.2 393.1 %all-reduce.3.cloned.1.call-start = ((), (), s32[]{:S(2)}) async-start(), calls=%async_computation | async-start | bytes 2129920 | tf_op jit(solution)/shard_map/psum | solution.py:146
  9.6 319.7 %collective-permute-start = (s32[8]{0:T(128)S(1)}, s32[8]{0:T(128)S(1)}, u32[]{:S(2)}, u32[]{:S(2)}) collective-permute-start(s32[8]{0:T(128)S(1)} %get-tuple-element.44), channel_id=1, source_target_pairs={{0,1},{1,2},{2,3},{3,4},{4,5},{5,6},{6,7},{7,0},{8,9},{9,10},{10,1... | collective-permute-start | bytes 104 | tf_op jit(solution)/shard_map/ppermute | solution.py:13
  10.1 319.5 %collective-permute-start.1 = (s32[8]{0:T(128)S(1)}, s32[8]{0:T(128)S(1)}, u32[]{:S(2)}, u32[]{:S(2)}) collective-permute-start(s32[8]{0:T(128)S(1)} %get-tuple-element.43), channel_id=1, source_target_pairs={{0,2},{1,3},{2,4},{3,5},{4,6},{5,7},{6,0},{7,1},{8,10},{9,11},{10,... | collective-permute-start | bytes 104 | tf_op jit(solution)/shard_map/ppermute | solution.py:13
  242.8 15.9 %copy-start.5 = (bf16[8,31]{1,0:T(8,128)(2,1)S(1)}, bf16[8,31]{1,0:T(8,128)(2,1)}, u32[]{:S(2)}) copy-start(bf16[8,31]{1,0:T(8,128)(2,1)} %param.16) | copy-start | bytes 1492
  323.1 0.9 copy-start.2
  323.1 0.9 copy-start.3
  325.3 4.5 %collective-permute-start.4 = (bf16[8,16,128]{2,1,0:T(8,128)(2,1)S(1)}, bf16[8,16,128]{2,1,0:T(8,128)(2,1)S(1)}, u32[]{:S(2)}, u32[]{:S(2)}) collective-permute-start(bf16[8,16,128]{2,1,0:T(8,128)(2,1)S(1)} %get-tuple-element.35), channel_id=1, source_target_pairs={{0,1},{1,2},{2,3},{3,4},{4,5},{5,6},{6,7},{7,0},{8,9},{9,10},{10,1... | collective-permute-start | bytes 98312 | tf_op jit(solution)/shard_map/ppermute | solution.py:13
  326.6 4.8 %collective-permute-start.5 = (bf16[8,16,128]{2,1,0:T(8,128)(2,1)S(1)}, bf16[8,16,128]{2,1,0:T(8,128)(2,1)S(1)}, u32[]{:S(2)}, u32[]{:S(2)}) collective-permute-start(bf16[8,16,128]{2,1,0:T(8,128)(2,1)S(1)} %get-tuple-element.34), channel_id=1, source_target_pairs={{0,2},{1,3},{2,4},{3,5},{4,6},{5,7},{6,0},{7,1},{8,10},{9,11},{10,... | collective-permute-start | bytes 98312 | tf_op jit(solution)/shard_map/ppermute | solution.py:13
  329.2 4.5 %collective-permute-start.2 = (bf16[8,16,128]{2,1,0:T(8,128)(2,1)S(1)}, bf16[8,16,128]{2,1,0:T(8,128)(2,1)S(1)}, u32[]{:S(2)}, u32[]{:S(2)}) collective-permute-start(bf16[8,16,128]{2,1,0:T(8,128)(2,1)S(1)} %get-tuple-element.38), channel_id=1, source_target_pairs={{0,1},{1,2},{2,3},{3,4},{4,5},{5,6},{6,7},{7,0},{8,9},{9,10},{10,1... | collective-permute-start | bytes 98312 | tf_op jit(solution)/shard_map/ppermute | solution.py:13
  329.3 4.9 %collective-permute-start.3 = (bf16[8,16,128]{2,1,0:T(8,128)(2,1)S(1)}, bf16[8,16,128]{2,1,0:T(8,128)(2,1)S(1)}, u32[]{:S(2)}, u32[]{:S(2)}) collective-permute-start(bf16[8,16,128]{2,1,0:T(8,128)(2,1)S(1)} %get-tuple-element.37), channel_id=1, source_target_pairs={{0,2},{1,3},{2,4},{3,5},{4,6},{5,7},{6,0},{7,1},{8,10},{9,11},{10,... | collective-permute-start | bytes 98312 | tf_op jit(solution)/shard_map/ppermute | solution.py:13
  336.5 2.7 collective-permute-start.6
  339.2 3.1 collective-permute-start.7
  400.3 5.4 %copy-start.1 = (f32[2,1040,128]{2,1,0:T(8,128)S(1)}, f32[2,1040,128]{2,1,0:T(8,128)}, u32[]{:S(2)}) copy-start(f32[2,1040,128]{2,1,0:T(8,128)} %all-reduce.3.cloned.1.call-done) | copy-start | bytes 3194884
  403.1 3.7 collective-permute-start.8
  405.1 3.9 collective-permute-start.9
Sparse Core Ops, SparseCore 0:
  343.5 56.7 all-reduce.2
where the time goes:
time: 418 us; the launch traced here: 417 us
  local copies, waits for them, and re-layouts  317 us (76%)
  waiting for transfers between devices  63.8 us (15%)
  between operations  14.4 us (3%)
  starting transfers between devices  11.9 us (3%)
  other arithmetic  9.12 us (2%)
    gather x4, local copies, waits for them, and re-layouts, toeplitz(): band_table = jnp.take(kernel_taps, tap_index, axis=1)  309 us
    psum x1, waiting for transfers between devices, body(): totals = lax.psum(extended, 'exp')  56.9 us
    ppermute x8, starting transfers between devices, shifted(): lax.ppermute(shard, axis, [(i, (i + by) % length) for i in range(length)])  8.77 us
  transfers between devices with their start and end apart: 11, of which 7 were waited for; matrix products, arithmetic and copies ran while one was open for 76% of the time, Pallas kernels for 0%

commit v1 on v0

--- a/solution.py
+++ b/solution.py
@@ -143,7 +143,7 @@
     core_rows = core_rows.at[:, :rim_rows].add(padded[:, :rim_rows])
     core_rows = core_rows.at[:, TR : TR + rim_rows].add(padded[:, rim_rows + extent - 1 :])
     extended = jnp.concatenate([core_rows, jnp.zeros((2, 1, PC), jnp.float32)], axis=1)
-    totals = lax.psum(extended, "exp")
+    totals = jnp.sum(lax.all_gather(extended, "exp"), axis=0)
     template_ext = (totals[0] / jnp.maximum(totals[1], 1.0)).astype(jnp.bfloat16)
     cutout = template_ext[sky_row].reshape(reach, slot_count, PR, PC)
     returned_list = [cutout[0]]

time: 418 us -> 446 us (1.067)
  waiting for transfers between devices: 63.8 us -> 92.8 us
    all_gather x0 -> x1, waiting for transfers between devices: none -> 86 us  [body(): totals = jnp.sum(lax.all_gather(extended, 'exp'), axis=0)]
    psum x1 -> x0, waiting for transfers between devices: 56.9 us -> none  [body(): totals = lax.psum(extended, 'exp')]
  transfers between devices with their start and end apart: 11 -> 11, of which waited for: 7 -> 7; matrix products, arithmetic and copies ran while one was open for 76% -> 71% of each run, Pallas kernels for 0% -> 0%
where the time goes in v1:
time: 446 us; the launch traced here: 445 us
  local copies, waits for them, and re-layouts  315 us (71%)
  waiting for transfers between devices  92.8 us (21%)
  between operations  14.4 us (3%)
  starting transfers between devices  11.9 us (3%)
  other arithmetic  10.4 us (2%)
    gather x4, local copies, waits for them, and re-layouts, toeplitz(): band_table = jnp.take(kernel_taps, tap_index, axis=1)  307 us
    all_gather x1, waiting for transfers between devices, body(): totals = jnp.sum(lax.all_gather(extended, 'exp'), axis=0)  86 us
  transfers between devices with their start and end apart: 11, of which 7 were waited for; matrix products, arithmetic and copies ran while one was open for 71% of the time, Pallas kernels for 0%

profile of v1, /device:TPU:0, one launch (start us, length us, event | category | flops | bytes accessed | tf_op | source)
XLA Modules:
  0.0 445.4 jit_solution(11665477547122041004)
XLA Ops:
  7.2 0.7 bitcast_select_fusion
  8.2 0.7 fusion.64
  8.9 0.6 scatter_custom_fusion
  9.6 0.5 collective-permute-start
  10.1 2.5 collective-permute-start.1
  12.9 0.7 copy.33
  13.9 227.3 %gather_fusion.1 = bf16[65536,8]{1,0:T(8,128)(2,1)} fusion(bf16[8,31]{0,1:T(8,128)(2,1)S(1)} %copy.25, s32[65536]{0:T(1024)S(1)} %broadcast_clamp_fusion), kind=kCustom, calls=%fused_computation.1 | custom fusion | bytes 2359296 | tf_op jit(solution)/shard_map/jit(_take)/gather | solution.py:39
  241.2 15.9 %copy.26 = bf16[256,256,8]{0,1,2:T(8,128)(2,1)S(1)} copy(bf16[256,256,8]{2,1,0:T(8,128)(2,1)} %bitcast.93) | data formatting | bytes 2097152 | tf_op jit(solution)/shard_map/jit(_take)/gather | solution.py:39
  257.2 57.4 %gather_fusion = bf16[16384,8]{1,0:T(8,128)(2,1)} fusion(bf16[8,31]{0,1:T(8,128)(2,1)S(1)} %copy.23, s32[16384]{0:T(1024)S(1)} %fusion.44), kind=kCustom, calls=%fused_computation | custom fusion | bytes 589824 | tf_op jit(solution)/shard_map/jit(_take)/gather | solution.py:39
  314.6 6.3 %copy.24 = bf16[128,128,8]{0,1,2:T(8,128)(2,1)S(1)} copy(bf16[128,128,8]{2,1,0:T(8,128)(2,1)} %bitcast.100) | data formatting | bytes 524288 | tf_op jit(solution)/shard_map/jit(_take)/gather | solution.py:39
  321.1 0.8 fusion
  322.2 1.0 scatter_fusion.1
  323.3 1.3 collective-permute-start.4
  324.6 1.5 collective-permute-start.5
  326.1 1.0 scatter_fusion
  327.8 1.6 collective-permute-done.5
  329.4 2.3 scatter_custom_fusion.4
  332.2 2.3 scatter_custom_fusion.2
  334.5 1.8 collective-permute-start.6
  336.3 0.8 collective-permute-done.6
  337.2 1.3 collective-permute-start.7
  338.7 1.5 collective-permute-done.7
  340.2 1.0 concatenate.11
  341.3 86.0 %all-gather.3.cloned.1.call-done = f32[8,1040,128]{2,1,0:T(8,128)} async-done(((f32[2,1040,128]{2,1,0:T(8,128)}), f32[8,1040,128]{2,1,0:T(8,128)}) %all-gather.3.cloned.1.call-update) | async-done | bytes 4259856 | tf_op jit(solution)/shard_map/all_gather | solution.py:146
  427.3 2.5 reduce_sum.37
  430.0 1.4 gather_fusion.2
  431.5 1.7 collective-permute-start.8
  433.2 0.8 collective-permute-start.9
  434.0 0.7 slice_bitcast_fusion
  434.8 2.3 collective-permute-done.9
  437.2 0.6 gather_fusion.3
  438.0 0.6 fusion.39
  (68 shorter events, 3.4 us)
Async XLA Ops:
  7.2 313.9 %copy-start = (bf16[1,1,128,256]{3,2,1,0:T(8,128)(2,1)S(1)}, bf16[1,1,128,256]{3,2,1,0:T(8,128)(2,1)}, u32[]{:S(2)}) copy-start(bf16[1,1,128,256]{3,2,1,0:T(8,128)(2,1)} %param.12) | copy-start | bytes 196612
  7.2 6.6 %copy-start.3 = (bf16[8,31]{1,0:T(8,128)(2,1)S(1)}, bf16[8,31]{1,0:T(8,128)(2,1)}, u32[]{:S(2)}) copy-start(bf16[8,31]{1,0:T(8,128)(2,1)} %param.17) | copy-start | bytes 1492
  7.2 420.1 %all-gather.3.cloned.1.call-start = ((), (), s32[]{:S(2)}) async-start(), calls=%async_computation | async-start | bytes 5324800 | tf_op jit(solution)/shard_map/all_gather | solution.py:146
  9.6 317.7 %collective-permute-start = (s32[8]{0:T(128)S(1)}, s32[8]{0:T(128)S(1)}, u32[]{:S(2)}, u32[]{:S(2)}) collective-permute-start(s32[8]{0:T(128)S(1)} %get-tuple-element.44), channel_id=1, source_target_pairs={{0,1},{1,2},{2,3},{3,4},{4,5},{5,6},{6,7},{7,0},{8,9},{9,10},{10,1... | collective-permute-start | bytes 104 | tf_op jit(solution)/shard_map/ppermute | solution.py:13
  10.1 317.5 %collective-permute-start.1 = (s32[8]{0:T(128)S(1)}, s32[8]{0:T(128)S(1)}, u32[]{:S(2)}, u32[]{:S(2)}) collective-permute-start(s32[8]{0:T(128)S(1)} %get-tuple-element.43), channel_id=1, source_target_pairs={{0,2},{1,3},{2,4},{3,5},{4,6},{5,7},{6,0},{7,1},{8,10},{9,11},{10,... | collective-permute-start | bytes 104 | tf_op jit(solution)/shard_map/ppermute | solution.py:13
  241.2 15.9 %copy-start.4 = (bf16[8,31]{1,0:T(8,128)(2,1)S(1)}, bf16[8,31]{1,0:T(8,128)(2,1)}, u32[]{:S(2)}) copy-start(bf16[8,31]{1,0:T(8,128)(2,1)} %param.16) | copy-start | bytes 1492
  321.1 0.9 copy-start.1
  321.1 0.9 copy-start.2
  323.3 4.5 %collective-permute-start.4 = (bf16[8,16,128]{2,1,0:T(8,128)(2,1)S(1)}, bf16[8,16,128]{2,1,0:T(8,128)(2,1)S(1)}, u32[]{:S(2)}, u32[]{:S(2)}) collective-permute-start(bf16[8,16,128]{2,1,0:T(8,128)(2,1)S(1)} %get-tuple-element.35), channel_id=1, source_target_pairs={{0,1},{1,2},{2,3},{3,4},{4,5},{5,6},{6,7},{7,0},{8,9},{9,10},{10,1... | collective-permute-start | bytes 98312 | tf_op jit(solution)/shard_map/ppermute | solution.py:13
  324.6 4.8 %collective-permute-start.5 = (bf16[8,16,128]{2,1,0:T(8,128)(2,1)S(1)}, bf16[8,16,128]{2,1,0:T(8,128)(2,1)S(1)}, u32[]{:S(2)}, u32[]{:S(2)}) collective-permute-start(bf16[8,16,128]{2,1,0:T(8,128)(2,1)S(1)} %get-tuple-element.34), channel_id=1, source_target_pairs={{0,2},{1,3},{2,4},{3,5},{4,6},{5,7},{6,0},{7,1},{8,10},{9,11},{10,... | collective-permute-start | bytes 98312 | tf_op jit(solution)/shard_map/ppermute | solution.py:13
  327.2 4.5 %collective-permute-start.2 = (bf16[8,16,128]{2,1,0:T(8,128)(2,1)S(1)}, bf16[8,16,128]{2,1,0:T(8,128)(2,1)S(1)}, u32[]{:S(2)}, u32[]{:S(2)}) collective-permute-start(bf16[8,16,128]{2,1,0:T(8,128)(2,1)S(1)} %get-tuple-element.38), channel_id=1, source_target_pairs={{0,1},{1,2},{2,3},{3,4},{4,5},{5,6},{6,7},{7,0},{8,9},{9,10},{10,1... | collective-permute-start | bytes 98312 | tf_op jit(solution)/shard_map/ppermute | solution.py:13
  327.3 4.9 %collective-permute-start.3 = (bf16[8,16,128]{2,1,0:T(8,128)(2,1)S(1)}, bf16[8,16,128]{2,1,0:T(8,128)(2,1)S(1)}, u32[]{:S(2)}, u32[]{:S(2)}) collective-permute-start(bf16[8,16,128]{2,1,0:T(8,128)(2,1)S(1)} %get-tuple-element.37), channel_id=1, source_target_pairs={{0,2},{1,3},{2,4},{3,5},{4,6},{5,7},{6,0},{7,1},{8,10},{9,11},{10,... | collective-permute-start | bytes 98312 | tf_op jit(solution)/shard_map/ppermute | solution.py:13
  334.5 2.7 collective-permute-start.6
  337.2 3.1 collective-permute-start.7
  431.5 3.3 collective-permute-start.8
  433.2 3.9 collective-permute-start.9
Sparse Core Ops, SparseCore 0:
  341.4 85.8 all-gather.2
